TPU v7x, 128 devices: a whole 4x4x4 slice. The times are simulated.
128 devices in a mesh: seq: 32 (over x_hi, z, y), tensor: 2 (over core), dp: 2 (over x_lo).
Axes of the slice: x: 4 (x_hi: 2, x_lo: 2; x = x_hi * 2 + x_lo), y: 4, z: 4, core: 2. Of those that a mesh axis runs over, the one named last changes fastest.
Arguments:
- inputs: bfloat16 [2, 24576, 1536], P('dp', 'seq', 'tensor'), may hold values from -6 to 6
- lengths: int32 [2], P('dp'), may hold values from 6144 to 24576, as said below
- cotangent: bfloat16 [2, 24576, 1536], P('dp', 'seq', 'tensor'), may hold values from -6 to 6
- w_value: bfloat16 [1536, 1536], P(None, 'tensor'), may hold values from -0.15625 to 0.15625
- w_gate: bfloat16 [1536, 1536], P(None, 'tensor'), may hold values from -0.15625 to 0.15625
- kernel: bfloat16 [31, 1536], P(None, 'tensor'), may hold values from -1 to 1
- w_out: bfloat16 [1536, 1536], P('tensor'), may hold values from -0.15625 to 0.15625
Outputs:
- output: bfloat16 [2, 24576, 1536], P('dp', 'seq', 'tensor')
- input_gradient: bfloat16 [2, 24576, 1536], P('dp', 'seq', 'tensor')
- value_grad: float32 [1536, 1536], P(('seq', 'dp'), 'tensor')
- gate_grad: float32 [1536, 1536], P(('seq', 'dp'), 'tensor')
- kernel_grad: float32 [31, 1536], P(None, 'tensor')
- out_grad: float32 [1536, 1536], P('tensor', ('seq', 'dp'))
Inputs may be any that keep to these rules, and one draw needn't show every extreme that they name: `lengths`: in every draw some utterance has all 24576 frames valid.
All inputs are finite; a program needn't handle non-finite values.
Results may differ from a plain program's by a relative error of at most 0.009.
Values may be sent and summed in bfloat16 or wider, within the bound.
A program may use at most 128 MiB of HBM per device.

v0:
```python
import jax
import jax.numpy as jnp
from jax import lax
from jax.sharding import PartitionSpec as P

epsilon = 1e-05


def padded_2(shard, sides, width):
    for axis, dim in sides:
        peers, length = (lax.axis_size(axis), shard.shape[dim])
        up = [(i, (i + 1) % peers) for i in range(peers - 1)]
        down = [(j, i) for i, j in up]
        last = lax.slice_in_dim(shard, length - width, length, axis=dim)
        leading = lax.slice_in_dim(shard, 0, width, axis=dim)
        before = lax.ppermute(last, axis, up)
        after = lax.ppermute(leading, axis, down)
        shard = jnp.concatenate([before, shard, after], axis=dim)
    return shard


def layer_normalizer(values):
    center = values - jnp.mean(values, axis=-1, keepdims=True)
    inverse = lax.rsqrt(jnp.mean(center * center, axis=-1, keepdims=True) + epsilon)
    return (center * inverse, inverse)


def shards(inputs, lengths, cotangent, w_value, w_gate, kernel, w_out):
    frame_total = inputs[0]
    count = frame_total.shape[0]
    channel_total = frame_total.shape[1]
    channel_width = channel_total * lax.axis_size("tensor")
    taps_count = kernel.shape[0]
    half = (taps_count - 1) // 2
    tensor_position = lax.axis_index("tensor")
    first_frame = lax.axis_index("seq") * count
    positions = first_frame + jnp.arange(count, dtype=jnp.int32)
    valid = (positions < lengths[0]).astype(jnp.float32)[:, None]
    taps = kernel.astype(jnp.float32)
    complete_rows = lax.all_gather(frame_total, "tensor", axis=1, tiled=True)
    centered_scaled, inverse_deviation_one = layer_normalizer(complete_rows.astype(jnp.float32))
    normalized_rows = centered_scaled.astype(jnp.bfloat16)
    values = jnp.dot(normalized_rows, w_value, preferred_element_type=jnp.float32)
    gates = jnp.dot(normalized_rows, w_gate, preferred_element_type=jnp.float32)
    sigma = jax.nn.sigmoid(gates)
    hidden = (values * sigma * valid).astype(jnp.bfloat16)
    padded = padded_2(hidden, (("seq", 0),), half).astype(jnp.float32)
    conv = jnp.zeros((count, channel_total), jnp.float32)
    for offset in range(taps_count):
        conv = conv + padded[offset : offset + count] * taps[offset]
    conv_sum, conv_square = lax.psum(
        (jnp.sum(conv, axis=-1), jnp.sum(conv * conv, axis=-1)), "tensor"
    )
    conv_mean = (conv_sum / channel_width)[:, None]
    conv_var = (conv_square / channel_width)[:, None] - conv_mean * conv_mean
    rstd_two = lax.rsqrt(conv_var + epsilon)
    zhat = (conv - conv_mean) * rstd_two
    swish_gate = jax.nn.sigmoid(zhat)
    swished = (zhat * swish_gate).astype(jnp.bfloat16)
    partial_out = jnp.dot(swished, w_out, preferred_element_type=jnp.float32)
    summed = lax.psum_scatter(
        partial_out.astype(jnp.bfloat16), "tensor", scatter_dimension=1, tiled=True
    ).astype(jnp.float32)
    output = (frame_total.astype(jnp.float32) + summed).astype(jnp.bfloat16)
    upstream = cotangent[0]
    upstream_whole = lax.all_gather(upstream, "tensor", axis=1, tiled=True)
    out_term = jnp.dot(swished.T, upstream_whole, preferred_element_type=jnp.float32)
    dswish = jnp.dot(upstream_whole, w_out.T, preferred_element_type=jnp.float32)
    dswish = dswish * (swish_gate + zhat * swish_gate * (1.0 - swish_gate))
    slope_sum, slope_cross = lax.psum(
        (jnp.sum(dswish, axis=-1), jnp.sum(dswish * zhat, axis=-1)), "tensor"
    )
    dconv = rstd_two * (
        dswish
        - (slope_sum / channel_width)[:, None]
        - zhat * (slope_cross / channel_width)[:, None]
    )
    dconv = dconv.astype(jnp.bfloat16)
    slope = dconv.astype(jnp.float32)
    kernel_term = jnp.stack(
        [jnp.sum(padded[offset : offset + count] * slope, axis=0) for offset in range(taps_count)]
    )
    slope_pad = padded_2(dconv, (("seq", 0),), half).astype(jnp.float32)
    dhidden = jnp.zeros((count, channel_total), jnp.float32)
    for offset in range(taps_count):
        dhidden = dhidden + slope_pad[2 * half - offset : 2 * half - offset + count] * taps[offset]
    dhidden = dhidden * valid
    dvalues = (dhidden * sigma).astype(jnp.bfloat16)
    dgates = (dhidden * values * sigma * (1.0 - sigma)).astype(jnp.bfloat16)
    value_term = jnp.dot(normalized_rows.T, dvalues, preferred_element_type=jnp.float32)
    gate_term = jnp.dot(normalized_rows.T, dgates, preferred_element_type=jnp.float32)
    kernel_grad = lax.psum(kernel_term, ("seq", "dp"))
    dnormed_part = jnp.dot(dvalues, w_value.T, preferred_element_type=jnp.float32) + jnp.dot(
        dgates, w_gate.T, preferred_element_type=jnp.float32
    )
    normalized_grad = lax.psum_scatter(
        dnormed_part.astype(jnp.bfloat16), "tensor", scatter_dimension=1, tiled=True
    ).astype(jnp.float32)
    local_centered_scaled = lax.dynamic_slice_in_dim(
        centered_scaled, tensor_position * channel_total, channel_total, 1
    )
    input_total_sum, input_cross_term = lax.psum(
        (
            jnp.sum(normalized_grad, axis=-1),
            jnp.sum(normalized_grad * local_centered_scaled, axis=-1),
        ),
        "tensor",
    )
    input_gradient = upstream.astype(jnp.float32) + inverse_deviation_one * (
        normalized_grad
        - (input_total_sum / channel_width)[:, None]
        - local_centered_scaled * (input_cross_term / channel_width)[:, None]
    )
    input_gradient = input_gradient.astype(jnp.bfloat16)
    value_grad, gate_grad, out_grad = (
        lax.psum_scatter(value_term, ("seq", "dp"), scatter_dimension=0, tiled=True),
        lax.psum_scatter(gate_term, ("seq", "dp"), scatter_dimension=0, tiled=True),
        lax.psum_scatter(out_term, ("seq", "dp"), scatter_dimension=1, tiled=True),
    )
    return (output[None], input_gradient[None], value_grad, gate_grad, kernel_grad, out_grad)


def solution(mesh):
    return jax.shard_map(
        shards,
        mesh=mesh,
        in_specs=(
            P("dp", "seq", "tensor"),
            P("dp"),
            P("dp", "seq", "tensor"),
            P(None, "tensor"),
            P(None, "tensor"),
            P(None, "tensor"),
            P("tensor", None),
        ),
        out_specs=(
            P("dp", "seq", "tensor"),
            P("dp", "seq", "tensor"),
            P(("seq", "dp"), "tensor"),
            P(("seq", "dp"), "tensor"),
            P(None, "tensor"),
            P("tensor", ("seq", "dp")),
        ),
        check_vma=False,
    )
```

profile of v0, /device:TPU:0, one launch (start us, length us, event | category | flops | bytes accessed | tf_op | source)
XLA Modules:
  0.0 1369.6 jit_solution(1484095070607599668)
XLA Ops:
  7.2 0.7 all-gather.5.cloned.1.call-update
  8.0 0.7 all-gather.7.cloned.1.call-update
  9.4 0.2 slice_reduce_fusion.30
  9.8 16.1 %all-gather.5.cloned.1.call-done = bf16[1,768,1536]{2,1,0:T(8,128)(2,1)} async-done(((bf16[1,768,768]{2,1,0:T(8,128)(2,1)}), bf16[1,768,1536]{2,1,0:T(8,128)(2,1)}) %all-gather.5.cloned.1.call-update) | async-done | bytes 2359312 | tf_op jit(solution)/shard_map/all_gather | solution.py:40
  25.8 2.2 convert_reduce_fusion
  28.0 0.2 copy-done.2
  28.2 0.8 fusion.3
  29.0 2.3 add_divide_fusion.1
  31.4 3.5 multiply_convert_fusion.3
  34.9 3.5 collective-permute-start
  38.4 1.3 collective-permute-start.1
  39.7 0.1 slice_reduce_fusion.29
  39.9 4.2 collective-permute-done.1
  44.1 0.2 maximum_convert_fusion
  44.5 10.7 fusion.94
  55.4 2.5 all-reduce.2
  57.9 7.0 fusion.93
  64.9 2.5 all-reduce.1
  67.5 27.0 %fusion.39 = (f32[768]{0:T(1024)}, f32[768]{0:T(1024)}, f32[768]{0:T(1024)}, f32[768]{0:T(1024)}, f32[768]{0:T(1024)}, /*index=5*/f32[768]{0:T(1024)}, f32[768]{...) fusion(f32[798,768]{1,0:T(8,128)} %copy-done.1, ...), kind=kLoop, calls=%fused_computation.77 | loop fusion | flops 25938432 | bytes 48433152 | tf_op jit(solution)/shard_map/reduce_sum | solution.py:81
  94.5 0.6 fusion.96
  95.1 4.0 collective-permute-start.2
  99.0 1.3 collective-permute-start.3
  100.4 3.9 convolution_convert_fusion
  104.6 0.4 collective-permute-done.3
  105.1 1.1 maximum_convert_fusion.1
  106.5 10.9 multiply_convert_fusion
  117.4 0.4 multiply_convert_fusion.1
  117.8 2.0 fusion.98
  119.9 3.5 add_convert_fusion
  123.5 0.3 all-reduce.5.cloned.1.call-start
  123.9 15.4 %fusion.38 = (f32[768]{0:T(1024)S(1)}, f32[768]{0:T(1024)S(1)}, f32[768]{0:T(1024)S(1)}, f32[768]{0:T(1024)S(1)}, f32[768]{0:T(1024)S(1)}, /*index=5*/f32[768]{0...) fusion(bf16[768,768]{1,0:T(8,128)(2,1)S(1)} %get-tuple-element., ...), kind=kLoop, calls=%fused_computation.76 | loop fusion | flops 15915264 | bytes 31890432 | tf_op jit(solution)/shard_map/reduce_sum | solution.py:81
  139.9 2.6 stack.127
  142.6 7.1 fusion.72
  149.8 1.2 copy-done.9
  151.0 6.1 fusion.88
  157.1 1.2 copy-done.11
  158.3 6.1 fusion.86
  164.5 4.4 fusion.1
  169.0 2.6 fusion.80
  171.6 2.6 convert_reduce_fusion.1
  174.2 3.1 all-reduce
  177.2 0.7 broadcast_multiply_fusion
  177.9 3.6 fusion.81
  181.6 95.1 %all-reduce.5.cloned.1.call-done = f32[31,768]{1,0:T(8,128)} async-done(((f32[31,768]{1,0:T(8,128)}), f32[31,768]{1,0:T(8,128)}) %all-reduce.5.cloned.1.call-update) | async-done | bytes 95248 | tf_op jit(solution)/shard_map/psum | solution.py:92
  276.7 363.2 %reduce-scatter.14.cloned.1.call-done = f32[768,24]{0,1:T(8,128)} async-done(((f32[768,1536]{0,1:T(8,128)}), f32[768,24]{0,1:T(8,128)}) %reduce-scatter.14.cloned.1.call-update) | async-done | bytes 73744 | tf_op jit(solution)/shard_map/reduce_scatter | solution.py:118
  639.9 360.7 %reduce-scatter.10.cloned.1.call-done = f32[24,768]{1,0:T(8,128)} async-done(((f32[1536,768]{1,0:T(8,128)}), f32[24,768]{1,0:T(8,128)}) %reduce-scatter.10.cloned.1.call-update) | async-done | bytes 73744 | tf_op jit(solution)/shard_map/reduce_scatter | solution.py:116
  1000.6 360.6 %reduce-scatter.12.cloned.1.call-done = f32[24,768]{1,0:T(8,128)} async-done(((f32[1536,768]{1,0:T(8,128)}), f32[24,768]{1,0:T(8,128)}) %reduce-scatter.12.cloned.1.call-update) | async-done | bytes 73744 | tf_op jit(solution)/shard_map/reduce_scatter | solution.py:117
  1361.2 1.5 copy.15
  (250 shorter events, 1.1 us)
Async XLA Ops:
  7.2 24.2 %copy-start = (bf16[1536,768]{1,0:T(8,128)(2,1)S(1)}, bf16[1536,768]{1,0:T(8,128)(2,1)}, u32[]{:S(2)}) copy-start(bf16[1536,768]{1,0:T(8,128)(2,1)} %param.10) | copy-start | bytes 7077892
  7.2 18.6 %all-gather.5.cloned.1.call-start = ((), (), s32[]{:S(2)}) async-start(), calls=%async_computation.11 | async-start | bytes 3538944 | tf_op jit(solution)/shard_map/all_gather | solution.py:40
  7.9 50.0 %all-gather.7.cloned.1.call-start = ((), (), s32[]{:S(2)}) async-start(), calls=%async_computation.12 | async-start | bytes 3538944 | tf_op jit(solution)/shard_map/all_gather | solution.py:66
  8.7 160.3 %reduce-scatter.6.cloned.1.call-start = ((), (), s32[]{:S(2)}) async-start(), calls=%async_computation.5 | async-start | bytes 3538944 | tf_op jit(solution)/shard_map/reduce_scatter | solution.py:61
  9.6 34.8 %copy-start.13 = (f32[768]{0:T(1024)}, f32[768]{0:T(1024)S(1)}, u32[]{:S(2)}) copy-start(f32[768]{0:T(1024)S(1)} %get-tuple-element.47) | copy-start | bytes 9220
  9.6 34.8 %copy-start.15 = (f32[768]{0:T(1024)}, f32[768]{0:T(1024)S(1)}, u32[]{:S(2)}) copy-start(f32[768]{0:T(1024)S(1)} %get-tuple-element.48) | copy-start | bytes 9220
  9.6 34.8 %copy-start.17 = (f32[768]{0:T(1024)}, f32[768]{0:T(1024)S(1)}, u32[]{:S(2)}) copy-start(f32[768]{0:T(1024)S(1)} %get-tuple-element.49) | copy-start | bytes 9220
  9.6 34.8 %copy-start.19 = (f32[768]{0:T(1024)}, f32[768]{0:T(1024)S(1)}, u32[]{:S(2)}) copy-start(f32[768]{0:T(1024)S(1)} %get-tuple-element.50) | copy-start | bytes 9220
  9.6 34.8 %copy-start.21 = (f32[768]{0:T(1024)}, f32[768]{0:T(1024)S(1)}, u32[]{:S(2)}) copy-start(f32[768]{0:T(1024)S(1)} %get-tuple-element.51) | copy-start | bytes 9220
  9.6 34.8 %copy-start.23 = (f32[768]{0:T(1024)}, f32[768]{0:T(1024)S(1)}, u32[]{:S(2)}) copy-start(f32[768]{0:T(1024)S(1)} %get-tuple-element.52) | copy-start | bytes 9220
  9.6 34.8 %copy-start.25 = (f32[768]{0:T(1024)}, f32[768]{0:T(1024)S(1)}, u32[]{:S(2)}) copy-start(f32[768]{0:T(1024)S(1)} %get-tuple-element.53) | copy-start | bytes 9220
  9.6 34.8 %copy-start.27 = (f32[768]{0:T(1024)}, f32[768]{0:T(1024)S(1)}, u32[]{:S(2)}) copy-start(f32[768]{0:T(1024)S(1)} %get-tuple-element.54) | copy-start | bytes 9220
  9.7 34.8 %copy-start.29 = (f32[768]{0:T(1024)}, f32[768]{0:T(1024)S(1)}, u32[]{:S(2)}) copy-start(f32[768]{0:T(1024)S(1)} %get-tuple-element.55) | copy-start | bytes 9220
  9.7 34.8 %copy-start.31 = (f32[768]{0:T(1024)}, f32[768]{0:T(1024)S(1)}, u32[]{:S(2)}) copy-start(f32[768]{0:T(1024)S(1)} %get-tuple-element.56) | copy-start | bytes 9220
  9.7 34.8 %copy-start.33 = (f32[768]{0:T(1024)}, f32[768]{0:T(1024)S(1)}, u32[]{:S(2)}) copy-start(f32[768]{0:T(1024)S(1)} %get-tuple-element.57) | copy-start | bytes 9220
  9.7 34.8 %copy-start.35 = (f32[768]{0:T(1024)}, f32[768]{0:T(1024)S(1)}, u32[]{:S(2)}) copy-start(f32[768]{0:T(1024)S(1)} %get-tuple-element.58) | copy-start | bytes 9220
  9.7 34.8 %copy-start.37 = (f32[768]{0:T(1024)}, f32[768]{0:T(1024)S(1)}, u32[]{:S(2)}) copy-start(f32[768]{0:T(1024)S(1)} %get-tuple-element.59) | copy-start | bytes 9220
  9.7 34.8 %copy-start.39 = (f32[768]{0:T(1024)}, f32[768]{0:T(1024)S(1)}, u32[]{:S(2)}) copy-start(f32[768]{0:T(1024)S(1)} %get-tuple-element.60) | copy-start | bytes 9220
  9.7 34.8 %copy-start.41 = (f32[768]{0:T(1024)}, f32[768]{0:T(1024)S(1)}, u32[]{:S(2)}) copy-start(f32[768]{0:T(1024)S(1)} %get-tuple-element.61) | copy-start | bytes 9220
  9.7 21.6 %copy-start.71 = (f32[768]{0:T(1024)}, f32[768]{0:T(1024)S(1)}, u32[]{:S(2)}) copy-start(f32[768]{0:T(1024)S(1)} %fusion.82) | copy-start | bytes 9220
  34.9 5.0 collective-permute-start
  38.4 5.7 collective-permute-start.1
  67.4 32.9 %copy-start.3 = (f32[768,768]{1,0:T(8,128)S(1)}, f32[768,768]{1,0:T(8,128)}, u32[]{:S(2)}) copy-start(f32[768,768]{1,0:T(8,128)} %get-tuple-element.83) | copy-start | bytes 7077892
  67.4 32.9 %copy-start.92 = (f32[768]{0:T(1024)S(1)}, f32[768]{0:T(1024)}, u32[]{:S(2)}) copy-start(f32[768]{0:T(1024)} %copy-done.91) | copy-start | bytes 9220
  67.4 32.9 %copy-start.94 = (f32[768]{0:T(1024)S(1)}, f32[768]{0:T(1024)}, u32[]{:S(2)}) copy-start(f32[768]{0:T(1024)} %copy-done.93) | copy-start | bytes 9220
  67.4 32.9 %copy-start.95 = (bf16[768,1536]{1,0:T(8,128)(2,1)S(1)}, bf16[768,1536]{1,0:T(8,128)(2,1)}, u32[]{:S(2)}) copy-start(bf16[768,1536]{1,0:T(8,128)(2,1)} %param.13) | copy-start | bytes 7077892
  95.1 9.5 collective-permute-start.2
  99.0 6.0 collective-permute-start.3
  104.3 67.3 %reduce-scatter.8.cloned.1.call-start = ((), (), s32[]{:S(2)}) async-start(), calls=%async_computation.6 | async-start | bytes 3538944 | tf_op jit(solution)/shard_map/reduce_scatter | solution.py:96
  123.5 16.4 %copy-start.76 = (f32[768]{0:T(1024)S(1)}, f32[768]{0:T(1024)}, u32[]{:S(2)}) copy-start(f32[768]{0:T(1024)} %get-tuple-element.6) | copy-start | bytes 9220
  123.5 16.4 %copy-start.75 = (f32[768]{0:T(1024)S(1)}, f32[768]{0:T(1024)}, u32[]{:S(2)}) copy-start(f32[768]{0:T(1024)} %get-tuple-element.7) | copy-start | bytes 9220
  123.5 16.4 %copy-start.74 = (f32[768]{0:T(1024)S(1)}, f32[768]{0:T(1024)}, u32[]{:S(2)}) copy-start(f32[768]{0:T(1024)} %get-tuple-element.8) | copy-start | bytes 9220
  123.5 16.4 %copy-start.73 = (f32[768]{0:T(1024)S(1)}, f32[768]{0:T(1024)}, u32[]{:S(2)}) copy-start(f32[768]{0:T(1024)} %get-tuple-element.9) | copy-start | bytes 9220
  123.5 153.2 %all-reduce.5.cloned.1.call-start = ((), (), s32[]{:S(2)}) async-start(), calls=%async_computation.9 | async-start | bytes 196608 | tf_op jit(solution)/shard_map/psum | solution.py:92
  123.8 15.8 %copy-start.87 = (f32[768]{0:T(1024)S(1)}, f32[768]{0:T(1024)}, u32[]{:S(2)}) copy-start(f32[768]{0:T(1024)} %get-tuple-element.13) | copy-start | bytes 9220
  123.8 15.8 %copy-start.86 = (f32[768]{0:T(1024)S(1)}, f32[768]{0:T(1024)}, u32[]{:S(2)}) copy-start(f32[768]{0:T(1024)} %get-tuple-element.14) | copy-start | bytes 9220
  123.8 15.8 %copy-start.85 = (f32[768]{0:T(1024)S(1)}, f32[768]{0:T(1024)}, u32[]{:S(2)}) copy-start(f32[768]{0:T(1024)} %get-tuple-element.15) | copy-start | bytes 9220
  123.8 15.8 %copy-start.84 = (f32[768]{0:T(1024)S(1)}, f32[768]{0:T(1024)}, u32[]{:S(2)}) copy-start(f32[768]{0:T(1024)} %get-tuple-element.16) | copy-start | bytes 9220
  123.9 15.8 %copy-start.83 = (f32[768]{0:T(1024)S(1)}, f32[768]{0:T(1024)}, u32[]{:S(2)}) copy-start(f32[768]{0:T(1024)} %get-tuple-element.17) | copy-start | bytes 9220
  123.9 15.8 %copy-start.82 = (f32[768]{0:T(1024)S(1)}, f32[768]{0:T(1024)}, u32[]{:S(2)}) copy-start(f32[768]{0:T(1024)} %get-tuple-element.18) | copy-start | bytes 9220
  123.9 15.8 %copy-start.81 = (f32[768]{0:T(1024)S(1)}, f32[768]{0:T(1024)}, u32[]{:S(2)}) copy-start(f32[768]{0:T(1024)} %get-tuple-element.19) | copy-start | bytes 9220
  123.9 15.9 %copy-start.80 = (f32[768]{0:T(1024)S(1)}, f32[768]{0:T(1024)}, u32[]{:S(2)}) copy-start(f32[768]{0:T(1024)} %get-tuple-element.20) | copy-start | bytes 9220
  123.9 15.9 %copy-start.79 = (f32[768]{0:T(1024)S(1)}, f32[768]{0:T(1024)}, u32[]{:S(2)}) copy-start(f32[768]{0:T(1024)} %get-tuple-element.21) | copy-start | bytes 9220
  123.9 15.9 %copy-start.78 = (f32[768]{0:T(1024)S(1)}, f32[768]{0:T(1024)}, u32[]{:S(2)}) copy-start(f32[768]{0:T(1024)} %get-tuple-element.22) | copy-start | bytes 9220
  123.9 15.9 %copy-start.77 = (f32[768]{0:T(1024)S(1)}, f32[768]{0:T(1024)}, u32[]{:S(2)}) copy-start(f32[768]{0:T(1024)} %get-tuple-element.23) | copy-start | bytes 9220
  142.5 497.4 %reduce-scatter.14.cloned.1.call-start = ((), (), s32[]{:S(2)}) async-start(), calls=%async_computation.10 | async-start | bytes 4792320 | tf_op jit(solution)/shard_map/reduce_scatter | solution.py:118
  149.8 850.8 %reduce-scatter.10.cloned.1.call-start = ((), (), s32[]{:S(2)}) async-start(), calls=%async_computation.7 | async-start | bytes 4792320 | tf_op jit(solution)/shard_map/reduce_scatter | solution.py:116
  157.1 1204.1 %reduce-scatter.12.cloned.1.call-start = ((), (), s32[]{:S(2)}) async-start(), calls=%async_computation.8 | async-start | bytes 4792320 | tf_op jit(solution)/shard_map/reduce_scatter | solution.py:117
  (62 other events, 350.3 us)
Sparse Core Ops, SparseCore 0:
  9.7 16.1 all-gather.4
  27.5 14.9 all-gather.6
  104.4 19.5 reduce-scatter.5
  126.2 18.9 reduce-scatter.7
  150.3 126.3 all-reduce.4
  279.5 360.3 reduce-scatter.13
  642.9 357.6 reduce-scatter.9
  1003.5 357.6 reduce-scatter.11
where the time goes:
time: 1370 us
  waiting for transfers between devices  1200 us (88%)
  other arithmetic  82.8 us (6%)
  matrix products  41.6 us (3%)
  between operations  16.6 us (1%)
    reduce_scatter x1, waiting for transfers between devices, shards(): lax.psum_scatter(out_term, ('seq', 'dp'), scatter_dimension=1, tiled=True)  363 us
    reduce_scatter x1, waiting for transfers between devices, shards(): lax.psum_scatter(value_term, ('seq', 'dp'), scatter_dimension=0, tiled=True)  361 us
    reduce_scatter x1, waiting for transfers between devices, shards(): lax.psum_scatter(gate_term, ('seq', 'dp'), scatter_dimension=0, tiled=True)  361 us
    psum x1, waiting for transfers between devices, shards(): kernel_grad = lax.psum(kernel_term, ('seq', 'dp'))  95.1 us
    reduce_sum x2, other arithmetic, shards(): jnp.sum(padded[offset:offset + count] * slope, axis=0)  42.4 us
  transfers between devices with their start and end apart: 12, of which 7 were waited for; matrix products, arithmetic and copies ran while one was open for 7% of the time, Pallas kernels for 0%

commit v1 on v0

--- a/solution.py
+++ b/solution.py
@@ -89,7 +89,7 @@
     dgates = (dhidden * values * sigma * (1.0 - sigma)).astype(jnp.bfloat16)
     value_term = jnp.dot(normalized_rows.T, dvalues, preferred_element_type=jnp.float32)
     gate_term = jnp.dot(normalized_rows.T, dgates, preferred_element_type=jnp.float32)
-    kernel_grad = lax.psum(kernel_term, ("seq", "dp"))
+    kernel_grad = lax.psum(lax.psum(kernel_term, "seq"), "dp")
     dnormed_part = jnp.dot(dvalues, w_value.T, preferred_element_type=jnp.float32) + jnp.dot(
         dgates, w_gate.T, preferred_element_type=jnp.float32
     )

time: 1370 us -> 1610 us (1.18)
  waiting for transfers between devices: 1200 us -> 1430 us
  local copies, waits for them, and re-layouts: 8.21 us -> 30.3 us
    psum x1 -> x2, waiting for transfers between devices: 95.1 us -> 315 us  [shards(): kernel_grad = lax.psum(lax.psum(kernel_term, 'seq'), 'dp')]
    another operation x32, local copies, waits for them, and re-layouts: 2.72 us -> 23.7 us  [shards(): jnp.stack([jnp.sum(padded[offset:offset + count] * slope, axis=0) for off...]
  transfers between devices with their start and end apart: 12 -> 13, of which waited for: 7 -> 8; matrix products, arithmetic and copies ran while one was open for 7% -> 5% of each run, Pallas kernels for 0% -> 0%
where the time goes in v1:
time: 1610 us; the launch traced here: 1600 us
  waiting for transfers between devices  1430 us (89%)
  other arithmetic  70.7 us (4%)
  matrix products  43.7 us (3%)
  local copies, waits for them, and re-layouts  30.3 us (2%)
    reduce_scatter x1, waiting for transfers between devices, shards(): lax.psum_scatter(out_term, ('seq', 'dp'), scatter_dimension=1, tiled=True)  367 us
    reduce_scatter x1, waiting for transfers between devices, shards(): lax.psum_scatter(gate_term, ('seq', 'dp'), scatter_dimension=0, tiled=True)  361 us
    reduce_scatter x1, waiting for transfers between devices, shards(): lax.psum_scatter(value_term, ('seq', 'dp'), scatter_dimension=0, tiled=True)  361 us
    psum x2, waiting for transfers between devices, shards(): kernel_grad = lax.psum(lax.psum(kernel_term, 'seq'), 'dp')  315 us
  transfers between devices with their start and end apart: 13, of which 8 were waited for; matrix products, arithmetic and copies ran while one was open for 5% of the time, Pallas kernels for 0%

profile of v1, /device:TPU:0, one launch (start us, length us, event | category | flops | bytes accessed | tf_op | source)
XLA Modules:
  0.0 1604.3 jit_solution(5334378828020343096)
XLA Ops:
  7.2 0.7 all-gather.5.cloned.1.call-update
  8.0 0.7 all-gather.7.cloned.1.call-update
  9.4 0.7 slice_reduce_fusion.30
  10.8 15.1 all-gather.5.cloned.1.call-done
  25.8 2.2 convert_reduce_fusion
  28.2 0.8 fusion.3
  29.0 2.3 add_divide_fusion.1
  31.4 3.6 multiply_convert_fusion.3
  35.1 3.5 collective-permute-start
  38.6 1.3 collective-permute-start.1
  39.9 1.2 slice_reduce_fusion.29
  41.2 3.1 collective-permute-done.1
  44.7 10.8 fusion.94
  55.6 2.5 all-reduce.2
  58.2 7.0 fusion.93
  65.2 2.5 all-reduce.1
  67.7 25.7 %fusion.39 = (f32[768]{0:T(1024)S(1)}, f32[768]{0:T(1024)S(1)}, f32[768]{0:T(1024)S(1)}, f32[768]{0:T(1024)S(1)}, f32[768]{0:T(1024)S(1)}, /*index=5*/f32[768]{0...) fusion(f32[798,768]{1,0:T(8,128)} %copy-done.1, ...), kind=kLoop, calls=%fused_computation.77 | loop fusion | flops 25938432 | bytes 48433152 | tf_op jit(solution)/shard_map/reduce_sum | solution.py:81
  93.4 3.9 fusion.38
  97.2 0.6 fusion.96
  102.6 0.6 stack.122
  110.8 0.6 stack.109
  111.4 0.6 stack.110
  116.1 5.4 stack.127
  121.6 4.0 collective-permute-start.2
  125.6 1.3 collective-permute-start.3
  126.9 6.3 convolution_convert_fusion
  133.6 1.1 maximum_convert_fusion.1
  135.2 10.9 multiply_convert_fusion
  146.5 2.0 fusion.98
  148.5 3.6 add_convert_fusion
  152.4 293.5 %all-reduce.6.cloned.1.call-done = f32[31,768]{1,0:T(8,128)} async-done(((f32[31,768]{1,0:T(8,128)}), f32[31,768]{1,0:T(8,128)}) %all-reduce.6.cloned.1.call-update) | async-done | bytes 95248 | tf_op jit(solution)/shard_map/psum | solution.py:92
  446.0 6.8 fusion.72
  452.9 0.6 copy-done.43
  453.5 6.1 fusion.88
  459.6 1.2 copy-done.9
  460.8 6.1 fusion.86
  467.0 4.4 fusion.1
  471.5 2.8 fusion.80
  474.3 1.6 reduce-scatter.8.cloned.1.call-done
  475.9 2.5 convert_reduce_fusion.1
  478.4 3.1 all-reduce
  481.5 0.7 broadcast_multiply_fusion
  482.2 3.6 fusion.81
  485.9 21.5 %all-reduce.8.cloned.1.call-done = f32[31,768]{1,0:T(8,128)} async-done(((f32[31,768]{1,0:T(8,128)}), f32[31,768]{1,0:T(8,128)}) %all-reduce.8.cloned.1.call-update) | async-done | bytes 95248 | tf_op jit(solution)/shard_map/psum | solution.py:92
  507.3 367.1 %reduce-scatter.14.cloned.1.call-done = f32[768,24]{0,1:T(8,128)} async-done(((f32[768,1536]{0,1:T(8,128)}), f32[768,24]{0,1:T(8,128)}) %reduce-scatter.14.cloned.1.call-update) | async-done | bytes 73744 | tf_op jit(solution)/shard_map/reduce_scatter | solution.py:118
  874.5 360.9 %reduce-scatter.10.cloned.1.call-done = f32[24,768]{1,0:T(8,128)} async-done(((f32[1536,768]{1,0:T(8,128)}), f32[24,768]{1,0:T(8,128)}) %reduce-scatter.10.cloned.1.call-update) | async-done | bytes 73744 | tf_op jit(solution)/shard_map/reduce_scatter | solution.py:116
  1235.3 360.9 %reduce-scatter.12.cloned.1.call-done = f32[24,768]{1,0:T(8,128)} async-done(((f32[1536,768]{1,0:T(8,128)}), f32[24,768]{1,0:T(8,128)}) %reduce-scatter.12.cloned.1.call-update) | async-done | bytes 73744 | tf_op jit(solution)/shard_map/reduce_scatter | solution.py:117
  1596.2 1.5 copy.16
  (213 shorter events, 19.2 us)
Async XLA Ops:
  7.2 24.2 %copy-start = (bf16[1536,768]{1,0:T(8,128)(2,1)S(1)}, bf16[1536,768]{1,0:T(8,128)(2,1)}, u32[]{:S(2)}) copy-start(bf16[1536,768]{1,0:T(8,128)(2,1)} %param.10) | copy-start | bytes 7077892
  7.2 18.6 %all-gather.5.cloned.1.call-start = ((), (), s32[]{:S(2)}) async-start(), calls=%async_computation.12 | async-start | bytes 3538944 | tf_op jit(solution)/shard_map/all_gather | solution.py:40
  7.9 50.2 %all-gather.7.cloned.1.call-start = ((), (), s32[]{:S(2)}) async-start(), calls=%async_computation.13 | async-start | bytes 3538944 | tf_op jit(solution)/shard_map/all_gather | solution.py:66
  8.7 437.2 %all-reduce.6.cloned.1.call-start = ((), (), s32[]{:S(2)}) async-start(), calls=%async_computation.9 | async-start | bytes 196608 | tf_op jit(solution)/shard_map/psum | solution.py:92
  9.4 19.5 %copy-start.10 = (f32[31,768]{1,0:T(8,128)}, f32[31,768]{1,0:T(8,128)S(1)}, u32[]{:S(2)}) copy-start(f32[31,768]{1,0:T(8,128)S(1)} %convert_element_type.70) | copy-start | bytes 285700
  35.0 9.6 copy-start.12
  35.0 9.6 copy-start.14
  35.0 9.6 copy-start.16
  35.0 9.6 copy-start.18
  35.0 9.6 copy-start.20
  35.0 9.6 copy-start.22
  35.0 9.6 copy-start.24
  35.0 9.6 copy-start.26
  35.0 9.6 copy-start.28
  35.0 9.6 copy-start.30
  35.0 9.6 copy-start.32
  35.0 9.6 copy-start.34
  35.0 9.6 copy-start.36
  35.1 9.6 copy-start.38
  35.1 9.6 copy-start.40
  35.1 6.1 collective-permute-start
  38.6 5.7 collective-permute-start.1
  41.1 14.4 copy-start.44
  41.1 14.4 copy-start.46
  41.1 14.4 copy-start.48
  41.1 14.4 copy-start.50
  41.1 14.4 copy-start.52
  41.1 14.4 copy-start.54
  41.2 14.4 copy-start.56
  41.2 14.4 copy-start.58
  41.2 14.4 copy-start.60
  41.2 14.4 copy-start.62
  41.2 14.4 copy-start.64
  41.2 14.4 copy-start.66
  44.6 11.0 copy-start.1
  58.1 7.0 copy-start.72
  67.6 25.7 %copy-start.2 = (f32[798,768]{1,0:T(8,128)S(1)}, f32[798,768]{1,0:T(8,128)}, u32[]{:S(2)}) copy-start(f32[798,768]{1,0:T(8,128)} %copy-done.1) | copy-start | bytes 7354372
  121.6 349.9 %reduce-scatter.6.cloned.1.call-start = ((), (), s32[]{:S(2)}) async-start(), calls=%async_computation.5 | async-start | bytes 3538944 | tf_op jit(solution)/shard_map/reduce_scatter | solution.py:61
  121.6 11.9 collective-permute-start.2
  125.6 7.9 collective-permute-start.3
  133.2 342.7 %reduce-scatter.8.cloned.1.call-start = ((), (), s32[]{:S(2)}) async-start(), calls=%async_computation.6 | async-start | bytes 3538944 | tf_op jit(solution)/shard_map/reduce_scatter | solution.py:96
  152.1 293.9 %copy-start.73 = (f32[768]{0:T(1024)S(1)}, f32[768]{0:T(1024)}, u32[]{:S(2)}) copy-start(f32[768]{0:T(1024)} %copy-done.72) | copy-start | bytes 9220
  152.1 293.9 %copy-start.75 = (f32[768]{0:T(1024)S(1)}, f32[768]{0:T(1024)}, u32[]{:S(2)}) copy-start(f32[768]{0:T(1024)} %copy-done.74) | copy-start | bytes 9220
  152.1 355.2 %all-reduce.8.cloned.1.call-start = ((), (), s32[]{:S(2)}) async-start(), calls=%async_computation.10 | async-start | bytes 196608 | tf_op jit(solution)/shard_map/psum | solution.py:92
  445.9 428.5 %reduce-scatter.14.cloned.1.call-start = ((), (), s32[]{:S(2)}) async-start(), calls=%async_computation.11 | async-start | bytes 4792320 | tf_op jit(solution)/shard_map/reduce_scatter | solution.py:118
  452.9 782.5 %reduce-scatter.10.cloned.1.call-start = ((), (), s32[]{:S(2)}) async-start(), calls=%async_computation.7 | async-start | bytes 4792320 | tf_op jit(solution)/shard_map/reduce_scatter | solution.py:116
  459.6 1136.6 %reduce-scatter.12.cloned.1.call-start = ((), (), s32[]{:S(2)}) async-start(), calls=%async_computation.8 | async-start | bytes 4792320 | tf_op jit(solution)/shard_map/reduce_scatter | solution.py:117
  474.3 7.9 copy-start.7
  (43 other events, 85.5 us)
Sparse Core Ops, SparseCore 0:
  9.7 16.1 all-gather.4
  27.5 14.9 all-gather.6
  121.7 324.1 all-reduce.5
  448.1 11.4 reduce-scatter.5
  461.8 14.0 reduce-scatter.7
  478.2 29.0 all-reduce.7
  510.3 364.1 reduce-scatter.13
  877.4 357.8 reduce-scatter.9
  1238.3 357.8 reduce-scatter.11
